TPU v7x, 256 devices: a whole 4x4x8 slice. The times are simulated.
256 devices in a mesh: dom: 64 (over x, z, y_hi), head: 4 (over y_lo, core).
Axes of the slice: x: 4, y: 4 (y_hi: 2, y_lo: 2; y = y_hi * 2 + y_lo), z: 8, core: 2. Of those that a mesh axis runs over, the one named last changes fastest.
Arguments:
- vertex_embeddings: bfloat16 [32768, 512], P(('dom', 'head')), may hold values from -6 to 6
- adjacent_group_bank_ids: int32 [64, 4, 12], P('dom', 'head'), may hold values from -1 to 15, as said below
- coupling_strength_panels: bfloat16 [16, 128, 128], replicated, may hold values from -0.3125 to 0.3125
- asking_projector: bfloat16 [512, 512], replicated, may hold values from -0.25 to 0.25
- lookup_projector: bfloat16 [512, 512], replicated, may hold values from -0.25 to 0.25
- content_projector: bfloat16 [512, 512], replicated, may hold values from -0.25 to 0.25
- final_projector: bfloat16 [512, 512], replicated, may hold values from -0.25 to 0.25
- passing_inner_coefficients: bfloat16 [512, 1024], replicated, may hold values from -0.25 to 0.25
- passing_outer_coefficients: bfloat16 [1024, 512], replicated, may hold values from -0.1875 to 0.1875
- softness_per_subspace: float32 [8], replicated, may hold values from 0.5 to 2
- mixing_layer_gain: float32 [512], replicated, may hold values from 0.5 to 1.5
Outputs:
- result: bfloat16 [32768, 512], P(('dom', 'head'))
Inputs may be any that keep to these rules, and one draw needn't show every extreme that they name: `adjacent_group_bank_ids`: -1 marks a block without edges. The entry of a block for itself is never -1, nor is at least one entry for each neighbouring partition.
All inputs are finite; a program needn't handle non-finite values.
Results may differ from a plain program's by a relative error of at most 0.0054.
Values may be sent and summed in bfloat16 or wider, within the bound.
A program may use at most 64 MiB of HBM per device.

v0:
```python
import math
import jax
import jax.numpy as jnp
from jax import lax
from jax.sharding import Mesh
from jax.sharding import PartitionSpec as P

NUM_SUBSPACES = 8
SUBSPACE_WIDTH = 64
KEY_BLOCK = 2048
norm_eps = 1e-06
ROW = "x"
COLUMN = "z"
PAIR = "yhi"
DOM = (ROW, COLUMN, PAIR)
GROUP = (PAIR, "head")


def extended(shard, width):
    devices = lax.axis_size(ROW) * lax.axis_size(COLUMN) * lax.axis_size(PAIR)
    length = shard.shape[0]
    up = [(i, (i + 1) % devices) for i in range(devices - 1)]
    down = [(j, i) for i, j in up]
    last = lax.slice_in_dim(shard, length - width, length, axis=0)
    first = lax.slice_in_dim(shard, 0, width, axis=0)
    before = lax.ppermute(last, DOM, up)
    after = lax.ppermute(first, DOM, down)
    return jnp.concatenate([before, shard, after], axis=0)


def head_norm(projected, scales):
    rows = projected.shape[0]
    grouped = projected.reshape(rows, -1, SUBSPACE_WIDTH)
    mean_square = jnp.mean(grouped * grouped, axis=-1, keepdims=True)
    scaled = grouped * lax.rsqrt(mean_square + norm_eps)
    if scales is not None:
        scaled = scaled * scales[None, :, None]
    return scaled.reshape(rows, -1).astype(jnp.bfloat16)


def shards(
    vertex_embeddings,
    adjacent_group_bank_ids,
    coupling_strength_panels,
    asking_projector,
    lookup_projector,
    content_projector,
    final_projector,
    passing_inner_coefficients,
    passing_outer_coefficients,
    softness_per_subspace,
    mixing_layer_gain,
):
    block_len = vertex_embeddings.shape[0]
    group_size = lax.axis_size("head")
    pair_size = lax.axis_size(PAIR)
    members = group_size * pair_size
    slot_ids = adjacent_group_bank_ids.reshape(-1)
    halo_rows = extended(vertex_embeddings, block_len)
    me = lax.axis_index("head")
    gathered = [halo_rows]
    for shift in range(1, group_size):
        pairs = [(i, (i + shift) % group_size) for i in range(group_size)]
        gathered.append(lax.ppermute(halo_rows, "head", pairs))
    stacked = jnp.stack(gathered)
    order = (me - jnp.arange(group_size)) % group_size
    nearby = jnp.zeros_like(stacked).at[order].set(stacked).reshape(-1, halo_rows.shape[1])
    slot_order = slot_ids.reshape(3, group_size).T.reshape(-1)
    asking_vector_multiplier = softness_per_subspace / math.sqrt(SUBSPACE_WIDTH)
    queries = head_norm(
        jnp.dot(vertex_embeddings, asking_projector, preferred_element_type=jnp.float32),
        asking_vector_multiplier,
    )
    keys_all = head_norm(
        jnp.dot(vertex_embeddings, lookup_projector, preferred_element_type=jnp.float32), None
    )
    values_all = jnp.dot(
        vertex_embeddings, content_projector, preferred_element_type=jnp.float32
    ).astype(jnp.bfloat16)
    head_of = [j % group_size * pair_size + j // group_size for j in range(members)]
    member_of = [head_of.index(h) for h in range(NUM_SUBSPACES)]
    packed = jnp.stack(
        [
            t.reshape(block_len, NUM_SUBSPACES, SUBSPACE_WIDTH)
            for t in (queries, keys_all, values_all)
        ],
        axis=2,
    )[:, jnp.array(head_of)]
    packed = packed.reshape(block_len, -1)
    mine = lax.all_to_all(packed, GROUP, split_axis=1, concat_axis=0, tiled=True)
    query_rows = mine.shape[0]
    head_queries = mine[:, :SUBSPACE_WIDTH]
    key_values = mine[:, SUBSPACE_WIDTH:]
    selected = jnp.take(coupling_strength_panels, jnp.maximum(slot_order, 0), axis=0)
    selected = jnp.where((slot_order >= 0)[:, None, None], selected, jnp.zeros_like(selected))
    wide_tiles = jnp.transpose(selected, (1, 0, 2)).reshape(block_len, -1)
    aggregate = jnp.dot(wide_tiles, nearby, preferred_element_type=jnp.float32).astype(jnp.bfloat16)
    hidden = jax.nn.gelu(
        jnp.dot(aggregate, passing_inner_coefficients, preferred_element_type=jnp.float32)
    ).astype(jnp.bfloat16)
    local_term = jnp.dot(hidden, passing_outer_coefficients, preferred_element_type=jnp.float32)
    local_term, head_queries = lax.optimization_barrier((local_term, head_queries))
    kv_in = lax.all_gather(key_values, (ROW, COLUMN), axis=0, tiled=True)
    key_count = kv_in.shape[0]
    block_step = min(KEY_BLOCK, key_count)
    ones = jnp.ones((block_step, SUBSPACE_WIDTH), jnp.bfloat16)

    def accumulate(turn_index, totals):
        block = lax.dynamic_slice_in_dim(kv_in, turn_index * block_step, block_step, 0)
        scores = jnp.einsum(
            "qd,kd->qk", head_queries, block[:, :SUBSPACE_WIDTH], preferred_element_type=jnp.float32
        )
        weights = jnp.exp(scores).astype(jnp.bfloat16)
        widened = jnp.concatenate([block[:, SUBSPACE_WIDTH:], ones], axis=1)
        return totals + jnp.dot(weights, widened, preferred_element_type=jnp.float32)

    totals = lax.fori_loop(
        0,
        key_count // block_step,
        accumulate,
        jnp.zeros((query_rows, 2 * SUBSPACE_WIDTH), jnp.float32),
    )
    merged = (totals[:, :SUBSPACE_WIDTH] / totals[:, SUBSPACE_WIDTH : SUBSPACE_WIDTH + 1]).astype(
        jnp.bfloat16
    )
    back = lax.all_to_all(merged, GROUP, split_axis=0, concat_axis=1, tiled=True)
    node_heads = back.reshape(block_len, members, SUBSPACE_WIDTH)[:, jnp.array(member_of)]
    node_heads = node_heads.reshape(block_len, -1)
    attended = jnp.dot(node_heads, final_projector, preferred_element_type=jnp.float32)
    normed = (
        attended
        * lax.rsqrt(jnp.mean(attended * attended, axis=-1, keepdims=True) + norm_eps)
        * mixing_layer_gain
    )
    return (vertex_embeddings.astype(jnp.float32) + local_term + normed).astype(jnp.bfloat16)


def solution(mesh):
    n_dom, n_head = (mesh.shape["dom"], mesh.shape["head"])
    fine = Mesh(mesh.devices.reshape(n_dom // 16, 8, 2, n_head), (ROW, COLUMN, PAIR, "head"))
    in_specs = (
        P((ROW, COLUMN, PAIR, "head"), None),
        P(DOM, "head", None),
        P(),
        P(),
        P(),
        P(),
        P(),
        P(),
        P(),
        P(),
        P(),
    )
    out_specs = P((ROW, COLUMN, PAIR, "head"), None)
    return jax.shard_map(shards, mesh=fine, in_specs=in_specs, out_specs=out_specs, check_vma=False)
```

profile of v0, /device:TPU:1, one launch (start us, length us, event | category | flops | bytes accessed | tf_op | source)
XLA Modules:
  0.0 226.7 jit_solution(1230595181593717141)
XLA Ops:
  11.8 13.9 %all_to_all.35 = bf16[128,8,192]{0,2,1:T(8,128)(2,1)S(1)} all-to-all(bf16[128,8,192]{0,2,1:T(8,128)(2,1)S(1)} %bitcast.63), channel_id=1, replica_groups=mesh['x'=4,'z'=8,'yhi'=2,'head'=4] {'yhi','head'}, dimensions={1} | all-to-all | bytes 786432 | tf_op jit(solution)/shard_map/all_to_all | solution.py:90
  31.0 6.4 %collective-permute-done.1 = bf16[128,512]{1,0:T(8,128)(2,1)S(1)} collective-permute-done((bf16[128,512]{1,0:T(8,128)(2,1)S(1)}, bf16[128,512]{1,0:T(8,128)(2,1)S(1)}, u32[]{:S(2)}, u32[]{:S(2)}) %collective-permute-start.1) | collective-permute-done | bytes 131104 | tf_op jit(solution)/shard_map/ppermute | solution.py:27
  44.0 3.7 %collective-permute-done.2 = bf16[384,512]{1,0:T(8,128)(2,1)} collective-permute-done((bf16[384,512]{1,0:T(8,128)(2,1)S(1)}, bf16[384,512]{1,0:T(8,128)(2,1)}, u32[]{:S(2)}, u32[]{:S(2)}) %collective-permute-start.2) | collective-permute-done | bytes 393248 | tf_op jit(solution)/shard_map/ppermute | solution.py:64
  47.7 10.4 %collective-permute-done.3 = bf16[384,512]{1,0:T(8,128)(2,1)} collective-permute-done((bf16[384,512]{1,0:T(8,128)(2,1)S(1)}, bf16[384,512]{1,0:T(8,128)(2,1)}, u32[]{:S(2)}, u32[]{:S(2)}) %collective-permute-start.3) | collective-permute-done | bytes 393248 | tf_op jit(solution)/shard_map/ppermute | solution.py:64
  61.7 4.7 %scatter_fusion = bf16[4,384,512]{2,1,0:T(8,128)(2,1)} fusion(bf16[4,384,512]{2,1,0:T(8,128)(2,1)} %broadcast_in_dim.47, s32[4]{0:T(128)S(1)} %fusion.20, bf16[4,384,512]{2,1,0:T(8,128)(2,1)S(1)} %pad_maximum_fusion), kind=kCustom, calls=%fused_computation.3 | custom fusion | bytes 4718608 | tf_op jit(solution)/shard_map/scatter | solution.py:67
  69.8 56.1 %all-gather.2.cloned.1.call-done = bf16[32768,128]{0,1:T(8,128)(2,1)} async-done(((bf16[1024,128]{0,1:T(8,128)(2,1)}), bf16[32768,128]{0,1:T(8,128)(2,1)}) %all-gather.2.cloned.1.call-update) | async-done | bytes 8388624 | tf_op jit(solution)/shard_map/all_gather | solution.py:103
  125.9 80.3 %while.14 = (s32[]{:T(128)}, f32[1024,128]{1,0:T(8,128)S(1)}, bf16[32768,128]{0,1:T(8,128)(2,1)}, bf16[1024,64]{1,0:T(8,128)(2,1)S(1)}, s32[]{:T(128)}, /*index=5*/s32[]{:T(128)}, s32[]{:T(128)}, s32[]{:T(128)}, s32[]{}) while((s32[]{:T(128)}, f32[1024,128]{1,0:T(8,128)S(1)}, bf16[32768,128]{0,1:T(8,128)(2,1)}, ...), condition=%wide.region_4.5_spmd.clone, body=%wide.region_3.4_spmd.clone.sunk | while | flops 807665664 | bytes 2752681 | solution.py:117
  127.2 3.7 %fusion.47 = f32[1024,128]{1,0:T(8,128)S(1)} fusion(bf16[1024,64]{1,0:T(8,128)(2,1)S(1)} %get-tuple-element.180, f32[1024,128]{1,0:T(8,128)S(1)} %get-tuple-element.169, bf16[2048,64]{1,0:T(8,128)(2,1)S(1)} %copy.93, bf16[32768,128]{0,1:T(8,128)(2,1)} %get-tuple-element.179, s32[]{:T(128)S(6)} %select_n.73, pred[]{:T(512)S(6)} %compare.11), kind=kOutput, calls=%fused_computation.6.clone.1 | convolution fusion | flops 807665664 | bytes 1703941 | tf_op jit(solution)/shard_map/while/body/eval_jaxpr/dot_general | solution.py:115
  132.2 3.7 %fusion.47 = f32[1024,128]{1,0:T(8,128)S(1)} fusion(bf16[1024,64]{1,0:T(8,128)(2,1)S(1)} %get-tuple-element.180, f32[1024,128]{1,0:T(8,128)S(1)} %get-tuple-element.169, bf16[2048,64]{1,0:T(8,128)(2,1)S(1)} %copy.93, bf16[32768,128]{0,1:T(8,128)(2,1)} %get-tuple-element.179, s32[]{:T(128)S(6)} %select_n.73, pred[]{:T(512)S(6)} %compare.11), kind=kOutput, calls=%fused_computation.6.clone.1 | convolution fusion | flops 807665664 | bytes 1703941 | tf_op jit(solution)/shard_map/while/body/eval_jaxpr/dot_general | solution.py:115
  137.2 3.7 %fusion.47 = f32[1024,128]{1,0:T(8,128)S(1)} fusion(bf16[1024,64]{1,0:T(8,128)(2,1)S(1)} %get-tuple-element.180, f32[1024,128]{1,0:T(8,128)S(1)} %get-tuple-element.169, bf16[2048,64]{1,0:T(8,128)(2,1)S(1)} %copy.93, bf16[32768,128]{0,1:T(8,128)(2,1)} %get-tuple-element.179, s32[]{:T(128)S(6)} %select_n.73, pred[]{:T(512)S(6)} %compare.11), kind=kOutput, calls=%fused_computation.6.clone.1 | convolution fusion | flops 807665664 | bytes 1703941 | tf_op jit(solution)/shard_map/while/body/eval_jaxpr/dot_general | solution.py:115
  142.2 3.7 %fusion.47 = f32[1024,128]{1,0:T(8,128)S(1)} fusion(bf16[1024,64]{1,0:T(8,128)(2,1)S(1)} %get-tuple-element.180, f32[1024,128]{1,0:T(8,128)S(1)} %get-tuple-element.169, bf16[2048,64]{1,0:T(8,128)(2,1)S(1)} %copy.93, bf16[32768,128]{0,1:T(8,128)(2,1)} %get-tuple-element.179, s32[]{:T(128)S(6)} %select_n.73, pred[]{:T(512)S(6)} %compare.11), kind=kOutput, calls=%fused_computation.6.clone.1 | convolution fusion | flops 807665664 | bytes 1703941 | tf_op jit(solution)/shard_map/while/body/eval_jaxpr/dot_general | solution.py:115
  147.2 3.7 %fusion.47 = f32[1024,128]{1,0:T(8,128)S(1)} fusion(bf16[1024,64]{1,0:T(8,128)(2,1)S(1)} %get-tuple-element.180, f32[1024,128]{1,0:T(8,128)S(1)} %get-tuple-element.169, bf16[2048,64]{1,0:T(8,128)(2,1)S(1)} %copy.93, bf16[32768,128]{0,1:T(8,128)(2,1)} %get-tuple-element.179, s32[]{:T(128)S(6)} %select_n.73, pred[]{:T(512)S(6)} %compare.11), kind=kOutput, calls=%fused_computation.6.clone.1 | convolution fusion | flops 807665664 | bytes 1703941 | tf_op jit(solution)/shard_map/while/body/eval_jaxpr/dot_general | solution.py:115
  152.2 3.7 %fusion.47 = f32[1024,128]{1,0:T(8,128)S(1)} fusion(bf16[1024,64]{1,0:T(8,128)(2,1)S(1)} %get-tuple-element.180, f32[1024,128]{1,0:T(8,128)S(1)} %get-tuple-element.169, bf16[2048,64]{1,0:T(8,128)(2,1)S(1)} %copy.93, bf16[32768,128]{0,1:T(8,128)(2,1)} %get-tuple-element.179, s32[]{:T(128)S(6)} %select_n.73, pred[]{:T(512)S(6)} %compare.11), kind=kOutput, calls=%fused_computation.6.clone.1 | convolution fusion | flops 807665664 | bytes 1703941 | tf_op jit(solution)/shard_map/while/body/eval_jaxpr/dot_general | solution.py:115
  157.3 3.7 %fusion.47 = f32[1024,128]{1,0:T(8,128)S(1)} fusion(bf16[1024,64]{1,0:T(8,128)(2,1)S(1)} %get-tuple-element.180, f32[1024,128]{1,0:T(8,128)S(1)} %get-tuple-element.169, bf16[2048,64]{1,0:T(8,128)(2,1)S(1)} %copy.93, bf16[32768,128]{0,1:T(8,128)(2,1)} %get-tuple-element.179, s32[]{:T(128)S(6)} %select_n.73, pred[]{:T(512)S(6)} %compare.11), kind=kOutput, calls=%fused_computation.6.clone.1 | convolution fusion | flops 807665664 | bytes 1703941 | tf_op jit(solution)/shard_map/while/body/eval_jaxpr/dot_general | solution.py:115
  162.3 3.7 %fusion.47 = f32[1024,128]{1,0:T(8,128)S(1)} fusion(bf16[1024,64]{1,0:T(8,128)(2,1)S(1)} %get-tuple-element.180, f32[1024,128]{1,0:T(8,128)S(1)} %get-tuple-element.169, bf16[2048,64]{1,0:T(8,128)(2,1)S(1)} %copy.93, bf16[32768,128]{0,1:T(8,128)(2,1)} %get-tuple-element.179, s32[]{:T(128)S(6)} %select_n.73, pred[]{:T(512)S(6)} %compare.11), kind=kOutput, calls=%fused_computation.6.clone.1 | convolution fusion | flops 807665664 | bytes 1703941 | tf_op jit(solution)/shard_map/while/body/eval_jaxpr/dot_general | solution.py:115
  167.3 3.7 %fusion.47 = f32[1024,128]{1,0:T(8,128)S(1)} fusion(bf16[1024,64]{1,0:T(8,128)(2,1)S(1)} %get-tuple-element.180, f32[1024,128]{1,0:T(8,128)S(1)} %get-tuple-element.169, bf16[2048,64]{1,0:T(8,128)(2,1)S(1)} %copy.93, bf16[32768,128]{0,1:T(8,128)(2,1)} %get-tuple-element.179, s32[]{:T(128)S(6)} %select_n.73, pred[]{:T(512)S(6)} %compare.11), kind=kOutput, calls=%fused_computation.6.clone.1 | convolution fusion | flops 807665664 | bytes 1703941 | tf_op jit(solution)/shard_map/while/body/eval_jaxpr/dot_general | solution.py:115
  172.3 3.7 %fusion.47 = f32[1024,128]{1,0:T(8,128)S(1)} fusion(bf16[1024,64]{1,0:T(8,128)(2,1)S(1)} %get-tuple-element.180, f32[1024,128]{1,0:T(8,128)S(1)} %get-tuple-element.169, bf16[2048,64]{1,0:T(8,128)(2,1)S(1)} %copy.93, bf16[32768,128]{0,1:T(8,128)(2,1)} %get-tuple-element.179, s32[]{:T(128)S(6)} %select_n.73, pred[]{:T(512)S(6)} %compare.11), kind=kOutput, calls=%fused_computation.6.clone.1 | convolution fusion | flops 807665664 | bytes 1703941 | tf_op jit(solution)/shard_map/while/body/eval_jaxpr/dot_general | solution.py:115
  177.3 3.7 %fusion.47 = f32[1024,128]{1,0:T(8,128)S(1)} fusion(bf16[1024,64]{1,0:T(8,128)(2,1)S(1)} %get-tuple-element.180, f32[1024,128]{1,0:T(8,128)S(1)} %get-tuple-element.169, bf16[2048,64]{1,0:T(8,128)(2,1)S(1)} %copy.93, bf16[32768,128]{0,1:T(8,128)(2,1)} %get-tuple-element.179, s32[]{:T(128)S(6)} %select_n.73, pred[]{:T(512)S(6)} %compare.11), kind=kOutput, calls=%fused_computation.6.clone.1 | convolution fusion | flops 807665664 | bytes 1703941 | tf_op jit(solution)/shard_map/while/body/eval_jaxpr/dot_general | solution.py:115
  182.4 3.7 %fusion.47 = f32[1024,128]{1,0:T(8,128)S(1)} fusion(bf16[1024,64]{1,0:T(8,128)(2,1)S(1)} %get-tuple-element.180, f32[1024,128]{1,0:T(8,128)S(1)} %get-tuple-element.169, bf16[2048,64]{1,0:T(8,128)(2,1)S(1)} %copy.93, bf16[32768,128]{0,1:T(8,128)(2,1)} %get-tuple-element.179, s32[]{:T(128)S(6)} %select_n.73, pred[]{:T(512)S(6)} %compare.11), kind=kOutput, calls=%fused_computation.6.clone.1 | convolution fusion | flops 807665664 | bytes 1703941 | tf_op jit(solution)/shard_map/while/body/eval_jaxpr/dot_general | solution.py:115
  192.4 3.7 %fusion.47 = f32[1024,128]{1,0:T(8,128)S(1)} fusion(bf16[1024,64]{1,0:T(8,128)(2,1)S(1)} %get-tuple-element.180, f32[1024,128]{1,0:T(8,128)S(1)} %get-tuple-element.169, bf16[2048,64]{1,0:T(8,128)(2,1)S(1)} %copy.93, bf16[32768,128]{0,1:T(8,128)(2,1)} %get-tuple-element.179, s32[]{:T(128)S(6)} %select_n.73, pred[]{:T(512)S(6)} %compare.11), kind=kOutput, calls=%fused_computation.6.clone.1 | convolution fusion | flops 807665664 | bytes 1703941 | tf_op jit(solution)/shard_map/while/body/eval_jaxpr/dot_general | solution.py:115
  197.4 3.7 %fusion.47 = f32[1024,128]{1,0:T(8,128)S(1)} fusion(bf16[1024,64]{1,0:T(8,128)(2,1)S(1)} %get-tuple-element.180, f32[1024,128]{1,0:T(8,128)S(1)} %get-tuple-element.169, bf16[2048,64]{1,0:T(8,128)(2,1)S(1)} %copy.93, bf16[32768,128]{0,1:T(8,128)(2,1)} %get-tuple-element.179, s32[]{:T(128)S(6)} %select_n.73, pred[]{:T(512)S(6)} %compare.11), kind=kOutput, calls=%fused_computation.6.clone.1 | convolution fusion | flops 807665664 | bytes 1703941 | tf_op jit(solution)/shard_map/while/body/eval_jaxpr/dot_general | solution.py:115
  202.4 3.7 %fusion.47 = f32[1024,128]{1,0:T(8,128)S(1)} fusion(bf16[1024,64]{1,0:T(8,128)(2,1)S(1)} %get-tuple-element.180, f32[1024,128]{1,0:T(8,128)S(1)} %get-tuple-element.169, bf16[2048,64]{1,0:T(8,128)(2,1)S(1)} %copy.93, bf16[32768,128]{0,1:T(8,128)(2,1)} %get-tuple-element.179, s32[]{:T(128)S(6)} %select_n.73, pred[]{:T(512)S(6)} %compare.11), kind=kOutput, calls=%fused_computation.6.clone.1 | convolution fusion | flops 807665664 | bytes 1703941 | tf_op jit(solution)/shard_map/while/body/eval_jaxpr/dot_general | solution.py:115
  207.5 5.4 %all-to-all-start.1 = ((bf16[8,128,64]{1,2,0:T(8,128)(2,1)}), bf16[8,128,64]{1,2,0:T(8,128)(2,1)S(1)}, u32[]{:S(2)}, u32[]{:S(2)}) async-start(bf16[8,128,64]{1,2,0:T(8,128)(2,1)} %copy_bitcast_fusion.1), calls=%async_computation.1 | async-start | bytes 262144 | tf_op jit(solution)/shard_map/all_to_all | solution.py:126
  212.8 5.3 %all-to-all-done.1 = bf16[8,128,64]{1,2,0:T(8,128)(2,1)S(1)} async-done(((bf16[8,128,64]{1,2,0:T(8,128)(2,1)}), bf16[8,128,64]{1,2,0:T(8,128)(2,1)S(1)}, u32[]{:S(2)}, u32[]{:S(2)}) %all-to-all-start.1) | async-done | bytes 131104 | tf_op jit(solution)/shard_map/all_to_all | solution.py:126
  (128 shorter events, 50.4 us)
Async XLA Ops:
  6.5 59.8 %copy-start = (bf16[512,1024]{1,0:T(8,128)(2,1)S(1)}, bf16[512,1024]{1,0:T(8,128)(2,1)}, u32[]{:S(2)}) copy-start(bf16[512,1024]{1,0:T(8,128)(2,1)} %param.22) | copy-start | bytes 3145732
  6.5 2.8 %copy-start.11 = (f32[8]{0:T(128)S(1)}, f32[8]{0:T(128)}, u32[]{:S(2)}) copy-start(f32[8]{0:T(128)} %param.24) | copy-start | bytes 100
  6.5 119.4 %all-gather.2.cloned.1.call-start = ((), (), s32[]{:S(2)}) async-start(), calls=%async_computation.2 | async-start | bytes 8650752 | tf_op jit(solution)/shard_map/all_gather | solution.py:103
  7.6 2.1 copy-start.1
  7.6 2.1 copy-start.6
  9.7 1.0 copy-start.5
  10.1 1.0 copy-start.10
  11.8 28.8 %copy-start.12 = (s32[1,1,12]{2,1,0:T(1,128)S(1)}, s32[1,1,12]{2,1,0:T(1,128)}, u32[]{:S(2)}) copy-start(s32[1,1,12]{2,1,0:T(1,128)} %param.16) | copy-start | bytes 148
  25.7 18.2 %copy-start.2 = (bf16[1024,192]{0,1:T(8,128)(2,1)}, bf16[1024,192]{0,1:T(8,128)(2,1)S(1)}, u32[]{:S(2)}) copy-start(bf16[1024,192]{0,1:T(8,128)(2,1)S(1)} %copy_bitcast_fusion) | copy-start | bytes 1179652
  26.5 4.4 %collective-permute-start = (bf16[128,512]{1,0:T(8,128)(2,1)S(1)}, bf16[128,512]{1,0:T(8,128)(2,1)S(1)}, u32[]{:S(2)}, u32[]{:S(2)}) collective-permute-start(bf16[128,512]{1,0:T(8,128)(2,1)S(1)} %copy-done.1), channel_id=1, source_target_pairs={{0,4},{4,8},{8,12},{12,16},{16,20},{20,24},{24,28},{28,32},{32,36}... | collective-permute-start | bytes 393224 | tf_op jit(solution)/shard_map/ppermute | solution.py:26
  29.0 8.3 %collective-permute-start.1 = (bf16[128,512]{1,0:T(8,128)(2,1)S(1)}, bf16[128,512]{1,0:T(8,128)(2,1)S(1)}, u32[]{:S(2)}, u32[]{:S(2)}) collective-permute-start(bf16[128,512]{1,0:T(8,128)(2,1)S(1)} %copy-done.1), channel_id=1, source_target_pairs={{4,0},{8,4},{12,8},{16,12},{20,16},{24,20},{28,24},{32,28},{36,32}... | collective-permute-start | bytes 393224 | tf_op jit(solution)/shard_map/ppermute | solution.py:27
  37.4 21.4 %copy-start.4 = (bf16[384,512]{1,0:T(8,128)(2,1)}, bf16[384,512]{1,0:T(8,128)(2,1)S(1)}, u32[]{:S(2)}) copy-start(bf16[384,512]{1,0:T(8,128)(2,1)S(1)} %constant_dynamic-update-slice_fusion) | copy-start | bytes 1179652
  37.4 10.3 %collective-permute-start.2 = (bf16[384,512]{1,0:T(8,128)(2,1)S(1)}, bf16[384,512]{1,0:T(8,128)(2,1)}, u32[]{:S(2)}, u32[]{:S(2)}) collective-permute-start(bf16[384,512]{1,0:T(8,128)(2,1)S(1)} %constant_dynamic-update-slice_fusion), channel_id=1, source_target_pairs={{0,1},{1,2},{2,3},{3,0},{4,5},{5,6},{6,7},{7,4},{8,9},{9,10},{10,1... | collective-permute-start | bytes 1179656 | tf_op jit(solution)/shard_map/ppermute | solution.py:64
  39.4 18.7 %collective-permute-start.3 = (bf16[384,512]{1,0:T(8,128)(2,1)S(1)}, bf16[384,512]{1,0:T(8,128)(2,1)}, u32[]{:S(2)}, u32[]{:S(2)}) collective-permute-start(bf16[384,512]{1,0:T(8,128)(2,1)S(1)} %constant_dynamic-update-slice_fusion), channel_id=1, source_target_pairs={{0,2},{1,3},{2,0},{3,1},{4,6},{5,7},{6,4},{7,5},{8,10},{9,11},{10,... | collective-permute-start | bytes 1179656 | tf_op jit(solution)/shard_map/ppermute | solution.py:64
  40.6 18.2 %collective-permute-start.4 = (bf16[384,512]{1,0:T(8,128)(2,1)S(1)}, bf16[384,512]{1,0:T(8,128)(2,1)}, u32[]{:S(2)}, u32[]{:S(2)}) collective-permute-start(bf16[384,512]{1,0:T(8,128)(2,1)S(1)} %constant_dynamic-update-slice_fusion), channel_id=1, source_target_pairs={{0,3},{1,0},{2,1},{3,2},{4,7},{5,4},{6,5},{7,6},{8,11},{9,8},{10,9... | collective-permute-start | bytes 1179656 | tf_op jit(solution)/shard_map/ppermute | solution.py:64
  66.3 2.4 %copy-start.3 = (bf16[1024,512]{1,0:T(8,128)(2,1)S(1)}, bf16[1024,512]{1,0:T(8,128)(2,1)}, u32[]{:S(2)}) copy-start(bf16[1024,512]{1,0:T(8,128)(2,1)} %param.23) | copy-start | bytes 3145732
  68.7 0.9 slice-start
  206.2 6.7 %copy-start.9 = (s32[8]{0:T(128)S(1)}, s32[8]{0:T(128)}, u32[]{:S(2)}) copy-start(s32[8]{0:T(128)} %constant.122) | copy-start | bytes 100
  206.2 12.5 %copy-start.7 = (bf16[512,512]{1,0:T(8,128)(2,1)S(1)}, bf16[512,512]{1,0:T(8,128)(2,1)}, u32[]{:S(2)}) copy-start(bf16[512,512]{1,0:T(8,128)(2,1)} %param.21) | copy-start | bytes 1572868
  206.4 12.6 %copy-start.8 = (f32[512]{0:T(512)S(1)}, f32[512]{0:T(512)}, u32[]{:S(2)}) copy-start(f32[512]{0:T(512)} %param.25) | copy-start | bytes 6148
  207.5 10.6 %all-to-all-start.1 = ((bf16[8,128,64]{1,2,0:T(8,128)(2,1)}), bf16[8,128,64]{1,2,0:T(8,128)(2,1)S(1)}, u32[]{:S(2)}, u32[]{:S(2)}) async-start(bf16[8,128,64]{1,2,0:T(8,128)(2,1)} %copy_bitcast_fusion.1), calls=%async_computation.1 | async-start | bytes 262144 | tf_op jit(solution)/shard_map/all_to_all | solution.py:126
Sparse Core Ops, SparseCore 0:
  26.6 99.2 all-gather.1
where the time goes:
time: 228 us; the launch traced here: 227 us
  waiting for transfers between devices  83.2 us (36%)
  matrix products  64.5 us (28%)
  local copies, waits for them, and re-layouts  34.1 us (15%)
  blocking collectives  13.9 us (6%)
  between operations  13.8 us (6%)
  starting transfers between devices  12.4 us (5%)
  other arithmetic  4.14 us (2%)
    dot_general x16, matrix products, accumulate(): jnp.dot(weights, widened, preferred_element_type=jnp.float32)  59.7 us
    all_gather x1, waiting for transfers between devices, shards(): kv_in = lax.all_gather(key_values, (ROW, COLUMN), axis=0, tiled=True)  56.1 us
    slice x16, local copies, waits for them, and re-layouts, accumulate(): widened = jnp.concatenate([block[:, SUBSPACE_WIDTH:], ones], axis=1)  15.6 us
    ppermute x3, waiting for transfers between devices, shards(): gathered.append(lax.ppermute(halo_rows, 'head', pairs))  14.8 us
    all_to_all x1, blocking collectives, shards(): lax.all_to_all(packed, GROUP, split_axis=1, concat_axis=0, tiled=True)  13.9 us
    ppermute x1, waiting for transfers between devices, extended(): after = lax.ppermute(first, DOM, down)  6.36 us
    all_to_all x1, starting transfers between devices, shards(): lax.all_to_all(merged, GROUP, split_axis=0, concat_axis=1, tiled=True)  5.36 us
    all_to_all x1, waiting for transfers between devices, shards(): lax.all_to_all(merged, GROUP, split_axis=0, concat_axis=1, tiled=True)  5.26 us
  transfers between devices with their start and end apart: 7, of which 7 were waited for; matrix products, arithmetic and copies ran while one was open for 6% of the time, Pallas kernels for 0%

commit v1 on v0

--- a/solution.py
+++ b/solution.py
@@ -14,6 +14,13 @@
 PAIR = "yhi"
 DOM = (ROW, COLUMN, PAIR)
 GROUP = (PAIR, "head")
+
+
+def exchange_blocks(x, mesh_axis, split, join):
+    size = lax.axis_size(mesh_axis)
+    blocks = jnp.stack(jnp.split(x, size, axis=split), axis=0)
+    blocks = lax.all_to_all(blocks, mesh_axis, split_axis=0, concat_axis=0)
+    return jnp.concatenate(blocks, axis=join)
 
 
 def extended(shard, width):
@@ -123,7 +130,7 @@
     merged = (totals[:, :SUBSPACE_WIDTH] / totals[:, SUBSPACE_WIDTH : SUBSPACE_WIDTH + 1]).astype(
         jnp.bfloat16
     )
-    back = lax.all_to_all(merged, GROUP, split_axis=0, concat_axis=1, tiled=True)
+    back = exchange_blocks(merged, GROUP, 0, 1)
     node_heads = back.reshape(block_len, members, SUBSPACE_WIDTH)[:, jnp.array(member_of)]
     node_heads = node_heads.reshape(block_len, -1)
     attended = jnp.dot(node_heads, final_projector, preferred_element_type=jnp.float32)

time: 228 us -> 232 us (1.018)
  local copies, waits for them, and re-layouts: 34.1 us -> 39 us
    unnamed x29 -> x36, local copies, waits for them, and re-layouts: 0.52 us -> 4.8 us
where the time goes in v1:
time: 232 us; the launch traced here: 231 us
  waiting for transfers between devices  83.2 us (36%)
  matrix products  64.5 us (28%)
  local copies, waits for them, and re-layouts  39 us (17%)
  blocking collectives  13.9 us (6%)
  between operations  13.8 us (6%)
  starting transfers between devices  12.4 us (5%)
  other arithmetic  3.48 us (2%)
    dot_general x16, matrix products, accumulate(): jnp.dot(weights, widened, preferred_element_type=jnp.float32)  59.7 us
    all_gather x1, waiting for transfers between devices, shards(): kv_in = lax.all_gather(key_values, (ROW, COLUMN), axis=0, tiled=True)  56.1 us
    slice x16, local copies, waits for them, and re-layouts, accumulate(): widened = jnp.concatenate([block[:, SUBSPACE_WIDTH:], ones], axis=1)  15.6 us
    ppermute x3, waiting for transfers between devices, shards(): gathered.append(lax.ppermute(halo_rows, 'head', pairs))  14.8 us
    all_to_all x1, blocking collectives, shards(): lax.all_to_all(packed, GROUP, split_axis=1, concat_axis=0, tiled=True)  13.9 us
    ppermute x1, waiting for transfers between devices, extended(): after = lax.ppermute(first, DOM, down)  6.36 us
    all_to_all x1, starting transfers between devices, exchange_blocks(): blocks = lax.all_to_all(blocks, mesh_axis, split_axis=0, concat_axis=0)  5.36 us
    all_to_all x1, waiting for transfers between devices, exchange_blocks(): blocks = lax.all_to_all(blocks, mesh_axis, split_axis=0, concat_axis=0)  5.26 us
  transfers between devices with their start and end apart: 7, of which 7 were waited for; matrix products, arithmetic and copies ran while one was open for 6% of the time, Pallas kernels for 0%

profile of v1, /device:TPU:1, one launch (start us, length us, event | category | flops | bytes accessed | tf_op | source)
XLA Modules:
  0.0 230.9 jit_solution(11637859349614036254)
XLA Ops:
  11.8 13.9 %all_to_all.24 = bf16[128,8,192]{0,2,1:T(8,128)(2,1)S(1)} all-to-all(bf16[128,8,192]{0,2,1:T(8,128)(2,1)S(1)} %bitcast.90), channel_id=1, replica_groups=mesh['x'=4,'z'=8,'yhi'=2,'head'=4] {'yhi','head'}, dimensions={1} | all-to-all | bytes 786432 | tf_op jit(solution)/shard_map/all_to_all | solution.py:97
  31.0 6.4 %collective-permute-done.1 = bf16[128,512]{1,0:T(8,128)(2,1)S(1)} collective-permute-done((bf16[128,512]{1,0:T(8,128)(2,1)S(1)}, bf16[128,512]{1,0:T(8,128)(2,1)S(1)}, u32[]{:S(2)}, u32[]{:S(2)}) %collective-permute-start.1) | collective-permute-done | bytes 131104 | tf_op jit(solution)/shard_map/ppermute | solution.py:34
  44.0 3.7 %collective-permute-done.2 = bf16[384,512]{1,0:T(8,128)(2,1)} collective-permute-done((bf16[384,512]{1,0:T(8,128)(2,1)S(1)}, bf16[384,512]{1,0:T(8,128)(2,1)}, u32[]{:S(2)}, u32[]{:S(2)}) %collective-permute-start.2) | collective-permute-done | bytes 393248 | tf_op jit(solution)/shard_map/ppermute | solution.py:71
  47.7 10.4 %collective-permute-done.3 = bf16[384,512]{1,0:T(8,128)(2,1)} collective-permute-done((bf16[384,512]{1,0:T(8,128)(2,1)S(1)}, bf16[384,512]{1,0:T(8,128)(2,1)}, u32[]{:S(2)}, u32[]{:S(2)}) %collective-permute-start.3) | collective-permute-done | bytes 393248 | tf_op jit(solution)/shard_map/ppermute | solution.py:71
  61.7 4.7 %scatter_fusion = bf16[4,384,512]{2,1,0:T(8,128)(2,1)} fusion(bf16[4,384,512]{2,1,0:T(8,128)(2,1)} %broadcast_in_dim.47, s32[4]{0:T(128)S(1)} %fusion.19, bf16[4,384,512]{2,1,0:T(8,128)(2,1)S(1)} %pad_maximum_fusion), kind=kCustom, calls=%fused_computation.3 | custom fusion | bytes 4718608 | tf_op jit(solution)/shard_map/scatter | solution.py:74
  69.8 56.1 %all-gather.2.cloned.1.call-done = bf16[32768,128]{0,1:T(8,128)(2,1)} async-done(((bf16[1024,128]{0,1:T(8,128)(2,1)}), bf16[32768,128]{0,1:T(8,128)(2,1)}) %all-gather.2.cloned.1.call-update) | async-done | bytes 8388624 | tf_op jit(solution)/shard_map/all_gather | solution.py:110
  125.9 80.3 %while.14 = (s32[]{:T(128)}, f32[1024,128]{1,0:T(8,128)S(1)}, bf16[32768,128]{0,1:T(8,128)(2,1)}, bf16[1024,64]{1,0:T(8,128)(2,1)S(1)}, s32[]{:T(128)}, /*index=5*/s32[]{:T(128)}, s32[]{:T(128)}, s32[]{:T(128)}, s32[]{}) while((s32[]{:T(128)}, f32[1024,128]{1,0:T(8,128)S(1)}, bf16[32768,128]{0,1:T(8,128)(2,1)}, ...), condition=%wide.region_4.5_spmd.clone, body=%wide.region_3.4_spmd.clone.sunk | while | flops 807665664 | bytes 2752681 | solution.py:124
  127.2 3.7 %fusion.45 = f32[1024,128]{1,0:T(8,128)S(1)} fusion(bf16[1024,64]{1,0:T(8,128)(2,1)S(1)} %get-tuple-element.172, f32[1024,128]{1,0:T(8,128)S(1)} %get-tuple-element.161, bf16[2048,64]{1,0:T(8,128)(2,1)S(1)} %copy.54, bf16[32768,128]{0,1:T(8,128)(2,1)} %get-tuple-element.171, s32[]{:T(128)S(6)} %select_n.73, pred[]{:T(512)S(6)} %compare.11), kind=kOutput, calls=%fused_computation.6.clone.1 | convolution fusion | flops 807665664 | bytes 1703941 | tf_op jit(solution)/shard_map/while/body/eval_jaxpr/dot_general | solution.py:122
  132.2 3.7 %fusion.45 = f32[1024,128]{1,0:T(8,128)S(1)} fusion(bf16[1024,64]{1,0:T(8,128)(2,1)S(1)} %get-tuple-element.172, f32[1024,128]{1,0:T(8,128)S(1)} %get-tuple-element.161, bf16[2048,64]{1,0:T(8,128)(2,1)S(1)} %copy.54, bf16[32768,128]{0,1:T(8,128)(2,1)} %get-tuple-element.171, s32[]{:T(128)S(6)} %select_n.73, pred[]{:T(512)S(6)} %compare.11), kind=kOutput, calls=%fused_computation.6.clone.1 | convolution fusion | flops 807665664 | bytes 1703941 | tf_op jit(solution)/shard_map/while/body/eval_jaxpr/dot_general | solution.py:122
  137.2 3.7 %fusion.45 = f32[1024,128]{1,0:T(8,128)S(1)} fusion(bf16[1024,64]{1,0:T(8,128)(2,1)S(1)} %get-tuple-element.172, f32[1024,128]{1,0:T(8,128)S(1)} %get-tuple-element.161, bf16[2048,64]{1,0:T(8,128)(2,1)S(1)} %copy.54, bf16[32768,128]{0,1:T(8,128)(2,1)} %get-tuple-element.171, s32[]{:T(128)S(6)} %select_n.73, pred[]{:T(512)S(6)} %compare.11), kind=kOutput, calls=%fused_computation.6.clone.1 | convolution fusion | flops 807665664 | bytes 1703941 | tf_op jit(solution)/shard_map/while/body/eval_jaxpr/dot_general | solution.py:122
  142.2 3.7 %fusion.45 = f32[1024,128]{1,0:T(8,128)S(1)} fusion(bf16[1024,64]{1,0:T(8,128)(2,1)S(1)} %get-tuple-element.172, f32[1024,128]{1,0:T(8,128)S(1)} %get-tuple-element.161, bf16[2048,64]{1,0:T(8,128)(2,1)S(1)} %copy.54, bf16[32768,128]{0,1:T(8,128)(2,1)} %get-tuple-element.171, s32[]{:T(128)S(6)} %select_n.73, pred[]{:T(512)S(6)} %compare.11), kind=kOutput, calls=%fused_computation.6.clone.1 | convolution fusion | flops 807665664 | bytes 1703941 | tf_op jit(solution)/shard_map/while/body/eval_jaxpr/dot_general | solution.py:122
  147.2 3.7 %fusion.45 = f32[1024,128]{1,0:T(8,128)S(1)} fusion(bf16[1024,64]{1,0:T(8,128)(2,1)S(1)} %get-tuple-element.172, f32[1024,128]{1,0:T(8,128)S(1)} %get-tuple-element.161, bf16[2048,64]{1,0:T(8,128)(2,1)S(1)} %copy.54, bf16[32768,128]{0,1:T(8,128)(2,1)} %get-tuple-element.171, s32[]{:T(128)S(6)} %select_n.73, pred[]{:T(512)S(6)} %compare.11), kind=kOutput, calls=%fused_computation.6.clone.1 | convolution fusion | flops 807665664 | bytes 1703941 | tf_op jit(solution)/shard_map/while/body/eval_jaxpr/dot_general | solution.py:122
  152.2 3.7 %fusion.45 = f32[1024,128]{1,0:T(8,128)S(1)} fusion(bf16[1024,64]{1,0:T(8,128)(2,1)S(1)} %get-tuple-element.172, f32[1024,128]{1,0:T(8,128)S(1)} %get-tuple-element.161, bf16[2048,64]{1,0:T(8,128)(2,1)S(1)} %copy.54, bf16[32768,128]{0,1:T(8,128)(2,1)} %get-tuple-element.171, s32[]{:T(128)S(6)} %select_n.73, pred[]{:T(512)S(6)} %compare.11), kind=kOutput, calls=%fused_computation.6.clone.1 | convolution fusion | flops 807665664 | bytes 1703941 | tf_op jit(solution)/shard_map/while/body/eval_jaxpr/dot_general | solution.py:122
  157.3 3.7 %fusion.45 = f32[1024,128]{1,0:T(8,128)S(1)} fusion(bf16[1024,64]{1,0:T(8,128)(2,1)S(1)} %get-tuple-element.172, f32[1024,128]{1,0:T(8,128)S(1)} %get-tuple-element.161, bf16[2048,64]{1,0:T(8,128)(2,1)S(1)} %copy.54, bf16[32768,128]{0,1:T(8,128)(2,1)} %get-tuple-element.171, s32[]{:T(128)S(6)} %select_n.73, pred[]{:T(512)S(6)} %compare.11), kind=kOutput, calls=%fused_computation.6.clone.1 | convolution fusion | flops 807665664 | bytes 1703941 | tf_op jit(solution)/shard_map/while/body/eval_jaxpr/dot_general | solution.py:122
  162.3 3.7 %fusion.45 = f32[1024,128]{1,0:T(8,128)S(1)} fusion(bf16[1024,64]{1,0:T(8,128)(2,1)S(1)} %get-tuple-element.172, f32[1024,128]{1,0:T(8,128)S(1)} %get-tuple-element.161, bf16[2048,64]{1,0:T(8,128)(2,1)S(1)} %copy.54, bf16[32768,128]{0,1:T(8,128)(2,1)} %get-tuple-element.171, s32[]{:T(128)S(6)} %select_n.73, pred[]{:T(512)S(6)} %compare.11), kind=kOutput, calls=%fused_computation.6.clone.1 | convolution fusion | flops 807665664 | bytes 1703941 | tf_op jit(solution)/shard_map/while/body/eval_jaxpr/dot_general | solution.py:122
  167.3 3.7 %fusion.45 = f32[1024,128]{1,0:T(8,128)S(1)} fusion(bf16[1024,64]{1,0:T(8,128)(2,1)S(1)} %get-tuple-element.172, f32[1024,128]{1,0:T(8,128)S(1)} %get-tuple-element.161, bf16[2048,64]{1,0:T(8,128)(2,1)S(1)} %copy.54, bf16[32768,128]{0,1:T(8,128)(2,1)} %get-tuple-element.171, s32[]{:T(128)S(6)} %select_n.73, pred[]{:T(512)S(6)} %compare.11), kind=kOutput, calls=%fused_computation.6.clone.1 | convolution fusion | flops 807665664 | bytes 1703941 | tf_op jit(solution)/shard_map/while/body/eval_jaxpr/dot_general | solution.py:122
  172.3 3.7 %fusion.45 = f32[1024,128]{1,0:T(8,128)S(1)} fusion(bf16[1024,64]{1,0:T(8,128)(2,1)S(1)} %get-tuple-element.172, f32[1024,128]{1,0:T(8,128)S(1)} %get-tuple-element.161, bf16[2048,64]{1,0:T(8,128)(2,1)S(1)} %copy.54, bf16[32768,128]{0,1:T(8,128)(2,1)} %get-tuple-element.171, s32[]{:T(128)S(6)} %select_n.73, pred[]{:T(512)S(6)} %compare.11), kind=kOutput, calls=%fused_computation.6.clone.1 | convolution fusion | flops 807665664 | bytes 1703941 | tf_op jit(solution)/shard_map/while/body/eval_jaxpr/dot_general | solution.py:122
  177.3 3.7 %fusion.45 = f32[1024,128]{1,0:T(8,128)S(1)} fusion(bf16[1024,64]{1,0:T(8,128)(2,1)S(1)} %get-tuple-element.172, f32[1024,128]{1,0:T(8,128)S(1)} %get-tuple-element.161, bf16[2048,64]{1,0:T(8,128)(2,1)S(1)} %copy.54, bf16[32768,128]{0,1:T(8,128)(2,1)} %get-tuple-element.171, s32[]{:T(128)S(6)} %select_n.73, pred[]{:T(512)S(6)} %compare.11), kind=kOutput, calls=%fused_computation.6.clone.1 | convolution fusion | flops 807665664 | bytes 1703941 | tf_op jit(solution)/shard_map/while/body/eval_jaxpr/dot_general | solution.py:122
  182.4 3.7 %fusion.45 = f32[1024,128]{1,0:T(8,128)S(1)} fusion(bf16[1024,64]{1,0:T(8,128)(2,1)S(1)} %get-tuple-element.172, f32[1024,128]{1,0:T(8,128)S(1)} %get-tuple-element.161, bf16[2048,64]{1,0:T(8,128)(2,1)S(1)} %copy.54, bf16[32768,128]{0,1:T(8,128)(2,1)} %get-tuple-element.171, s32[]{:T(128)S(6)} %select_n.73, pred[]{:T(512)S(6)} %compare.11), kind=kOutput, calls=%fused_computation.6.clone.1 | convolution fusion | flops 807665664 | bytes 1703941 | tf_op jit(solution)/shard_map/while/body/eval_jaxpr/dot_general | solution.py:122
  192.4 3.7 %fusion.45 = f32[1024,128]{1,0:T(8,128)S(1)} fusion(bf16[1024,64]{1,0:T(8,128)(2,1)S(1)} %get-tuple-element.172, f32[1024,128]{1,0:T(8,128)S(1)} %get-tuple-element.161, bf16[2048,64]{1,0:T(8,128)(2,1)S(1)} %copy.54, bf16[32768,128]{0,1:T(8,128)(2,1)} %get-tuple-element.171, s32[]{:T(128)S(6)} %select_n.73, pred[]{:T(512)S(6)} %compare.11), kind=kOutput, calls=%fused_computation.6.clone.1 | convolution fusion | flops 807665664 | bytes 1703941 | tf_op jit(solution)/shard_map/while/body/eval_jaxpr/dot_general | solution.py:122
  197.4 3.7 %fusion.45 = f32[1024,128]{1,0:T(8,128)S(1)} fusion(bf16[1024,64]{1,0:T(8,128)(2,1)S(1)} %get-tuple-element.172, f32[1024,128]{1,0:T(8,128)S(1)} %get-tuple-element.161, bf16[2048,64]{1,0:T(8,128)(2,1)S(1)} %copy.54, bf16[32768,128]{0,1:T(8,128)(2,1)} %get-tuple-element.171, s32[]{:T(128)S(6)} %select_n.73, pred[]{:T(512)S(6)} %compare.11), kind=kOutput, calls=%fused_computation.6.clone.1 | convolution fusion | flops 807665664 | bytes 1703941 | tf_op jit(solution)/shard_map/while/body/eval_jaxpr/dot_general | solution.py:122
  202.4 3.7 %fusion.45 = f32[1024,128]{1,0:T(8,128)S(1)} fusion(bf16[1024,64]{1,0:T(8,128)(2,1)S(1)} %get-tuple-element.172, f32[1024,128]{1,0:T(8,128)S(1)} %get-tuple-element.161, bf16[2048,64]{1,0:T(8,128)(2,1)S(1)} %copy.54, bf16[32768,128]{0,1:T(8,128)(2,1)} %get-tuple-element.171, s32[]{:T(128)S(6)} %select_n.73, pred[]{:T(512)S(6)} %compare.11), kind=kOutput, calls=%fused_computation.6.clone.1 | convolution fusion | flops 807665664 | bytes 1703941 | tf_op jit(solution)/shard_map/while/body/eval_jaxpr/dot_general | solution.py:122
  211.7 5.4 %all-to-all-start.1 = ((bf16[8,128,64]{1,2,0:T(8,128)(2,1)}), bf16[8,128,64]{1,2,0:T(8,128)(2,1)S(1)}, u32[]{:S(2)}, u32[]{:S(2)}) async-start(bf16[8,128,64]{1,2,0:T(8,128)(2,1)} %constant_dynamic-update-slice_fusion.3), calls=%async_computation.1 | async-start | bytes 262144 | tf_op jit(solution)/shard_map/all_to_all | solution.py:22
  217.1 5.3 %all-to-all-done.1 = bf16[8,128,64]{1,2,0:T(8,128)(2,1)S(1)} async-done(((bf16[8,128,64]{1,2,0:T(8,128)(2,1)}), bf16[8,128,64]{1,2,0:T(8,128)(2,1)S(1)}, u32[]{:S(2)}, u32[]{:S(2)}) %all-to-all-start.1) | async-done | bytes 131104 | tf_op jit(solution)/shard_map/all_to_all | solution.py:22
  (136 shorter events, 54.7 us)
Async XLA Ops:
  6.5 59.8 %copy-start = (bf16[512,1024]{1,0:T(8,128)(2,1)S(1)}, bf16[512,1024]{1,0:T(8,128)(2,1)}, u32[]{:S(2)}) copy-start(bf16[512,1024]{1,0:T(8,128)(2,1)} %param.22) | copy-start | bytes 3145732
  6.5 2.8 %copy-start.11 = (f32[8]{0:T(128)S(1)}, f32[8]{0:T(128)}, u32[]{:S(2)}) copy-start(f32[8]{0:T(128)} %param.24) | copy-start | bytes 100
  6.5 119.4 %all-gather.2.cloned.1.call-start = ((), (), s32[]{:S(2)}) async-start(), calls=%async_computation.2 | async-start | bytes 8650752 | tf_op jit(solution)/shard_map/all_gather | solution.py:110
  7.6 2.1 copy-start.1
  7.6 2.1 copy-start.6
  9.7 1.0 copy-start.5
  10.1 1.0 copy-start.10
  11.8 28.8 %copy-start.12 = (s32[1,1,12]{2,1,0:T(1,128)S(1)}, s32[1,1,12]{2,1,0:T(1,128)}, u32[]{:S(2)}) copy-start(s32[1,1,12]{2,1,0:T(1,128)} %param.16) | copy-start | bytes 148
  25.7 18.2 %copy-start.2 = (bf16[1024,192]{0,1:T(8,128)(2,1)}, bf16[1024,192]{0,1:T(8,128)(2,1)S(1)}, u32[]{:S(2)}) copy-start(bf16[1024,192]{0,1:T(8,128)(2,1)S(1)} %copy_bitcast_fusion) | copy-start | bytes 1179652
  26.5 4.4 %collective-permute-start = (bf16[128,512]{1,0:T(8,128)(2,1)S(1)}, bf16[128,512]{1,0:T(8,128)(2,1)S(1)}, u32[]{:S(2)}, u32[]{:S(2)}) collective-permute-start(bf16[128,512]{1,0:T(8,128)(2,1)S(1)} %copy-done.1), channel_id=1, source_target_pairs={{0,4},{4,8},{8,12},{12,16},{16,20},{20,24},{24,28},{28,32},{32,36}... | collective-permute-start | bytes 393224 | tf_op jit(solution)/shard_map/ppermute | solution.py:33
  29.0 8.3 %collective-permute-start.1 = (bf16[128,512]{1,0:T(8,128)(2,1)S(1)}, bf16[128,512]{1,0:T(8,128)(2,1)S(1)}, u32[]{:S(2)}, u32[]{:S(2)}) collective-permute-start(bf16[128,512]{1,0:T(8,128)(2,1)S(1)} %copy-done.1), channel_id=1, source_target_pairs={{4,0},{8,4},{12,8},{16,12},{20,16},{24,20},{28,24},{32,28},{36,32}... | collective-permute-start | bytes 393224 | tf_op jit(solution)/shard_map/ppermute | solution.py:34
  37.4 21.4 %copy-start.4 = (bf16[384,512]{1,0:T(8,128)(2,1)}, bf16[384,512]{1,0:T(8,128)(2,1)S(1)}, u32[]{:S(2)}) copy-start(bf16[384,512]{1,0:T(8,128)(2,1)S(1)} %constant_dynamic-update-slice_fusion) | copy-start | bytes 1179652
  37.4 10.3 %collective-permute-start.2 = (bf16[384,512]{1,0:T(8,128)(2,1)S(1)}, bf16[384,512]{1,0:T(8,128)(2,1)}, u32[]{:S(2)}, u32[]{:S(2)}) collective-permute-start(bf16[384,512]{1,0:T(8,128)(2,1)S(1)} %constant_dynamic-update-slice_fusion), channel_id=1, source_target_pairs={{0,1},{1,2},{2,3},{3,0},{4,5},{5,6},{6,7},{7,4},{8,9},{9,10},{10,1... | collective-permute-start | bytes 1179656 | tf_op jit(solution)/shard_map/ppermute | solution.py:71
  39.4 18.7 %collective-permute-start.3 = (bf16[384,512]{1,0:T(8,128)(2,1)S(1)}, bf16[384,512]{1,0:T(8,128)(2,1)}, u32[]{:S(2)}, u32[]{:S(2)}) collective-permute-start(bf16[384,512]{1,0:T(8,128)(2,1)S(1)} %constant_dynamic-update-slice_fusion), channel_id=1, source_target_pairs={{0,2},{1,3},{2,0},{3,1},{4,6},{5,7},{6,4},{7,5},{8,10},{9,11},{10,... | collective-permute-start | bytes 1179656 | tf_op jit(solution)/shard_map/ppermute | solution.py:71
  40.6 18.2 %collective-permute-start.4 = (bf16[384,512]{1,0:T(8,128)(2,1)S(1)}, bf16[384,512]{1,0:T(8,128)(2,1)}, u32[]{:S(2)}, u32[]{:S(2)}) collective-permute-start(bf16[384,512]{1,0:T(8,128)(2,1)S(1)} %constant_dynamic-update-slice_fusion), channel_id=1, source_target_pairs={{0,3},{1,0},{2,1},{3,2},{4,7},{5,4},{6,5},{7,6},{8,11},{9,8},{10,9... | collective-permute-start | bytes 1179656 | tf_op jit(solution)/shard_map/ppermute | solution.py:71
  66.3 2.4 %copy-start.3 = (bf16[1024,512]{1,0:T(8,128)(2,1)S(1)}, bf16[1024,512]{1,0:T(8,128)(2,1)}, u32[]{:S(2)}) copy-start(bf16[1024,512]{1,0:T(8,128)(2,1)} %param.23) | copy-start | bytes 3145732
  68.7 0.9 slice-start
  206.2 10.9 %copy-start.9 = (s32[8]{0:T(128)S(1)}, s32[8]{0:T(128)}, u32[]{:S(2)}) copy-start(s32[8]{0:T(128)} %constant.122) | copy-start | bytes 100
  206.2 16.7 %copy-start.7 = (bf16[512,512]{1,0:T(8,128)(2,1)S(1)}, bf16[512,512]{1,0:T(8,128)(2,1)}, u32[]{:S(2)}) copy-start(bf16[512,512]{1,0:T(8,128)(2,1)} %param.21) | copy-start | bytes 1572868
  206.4 16.9 %copy-start.8 = (f32[512]{0:T(512)S(1)}, f32[512]{0:T(512)}, u32[]{:S(2)}) copy-start(f32[512]{0:T(512)} %param.25) | copy-start | bytes 6148
  211.7 10.6 %all-to-all-start.1 = ((bf16[8,128,64]{1,2,0:T(8,128)(2,1)}), bf16[8,128,64]{1,2,0:T(8,128)(2,1)S(1)}, u32[]{:S(2)}, u32[]{:S(2)}) async-start(bf16[8,128,64]{1,2,0:T(8,128)(2,1)} %constant_dynamic-update-slice_fusion.3), calls=%async_computation.1 | async-start | bytes 262144 | tf_op jit(solution)/shard_map/all_to_all | solution.py:22
Sparse Core Ops, SparseCore 0:
  26.6 99.2 all-gather.1
